TPU v7x, 32 devices: a whole 2x2x4 slice. The times are simulated.
32 devices in a mesh: gx: 4 (over z), gy: 4 (over x, core), gz: 2 (over y).
Axes of the slice: x: 2, y: 2, z: 4, core: 2. Of those that a mesh axis runs over, the one named last changes fastest.
Arguments:
- features: float32 [4, 8, 2, 128, 256], P('gx', 'gy', 'gz'), may hold values from -82 to 82
- occupancy: int32 [4, 8, 2], P('gx', 'gy', 'gz'), may hold values from 1 to 128, as said below
- dest_bin: int32 [4, 8, 2], P('gx', 'gy', 'gz'), may hold values from 0 to 63, as said below
- query_weight: bfloat16 [256, 256], replicated, may hold values from -0.375 to 0.375
- key_weight: bfloat16 [256, 256], replicated, may hold values from -0.375 to 0.375
- value_weight: bfloat16 [256, 256], replicated, may hold values from -0.375 to 0.375
- out_weight: bfloat16 [256, 256], replicated, may hold values from -0.375 to 0.375
- up_weight: bfloat16 [256, 1024], replicated, may hold values from -0.375 to 0.375
- down_weight: bfloat16 [1024, 256], replicated, may hold values from -0.1875 to 0.1875
- attention_gain: float32 [256], replicated, may hold values from 0.25 to 1.75
- feed_gain: float32 [256], replicated, may hold values from 0.25 to 1.75
Outputs:
- particles: float32 [4, 8, 2, 128, 256], P('gx', 'gy', 'gz')
Inputs may be any that keep to these rules, and one draw needn't show every extreme that they name: `occupancy`: some bin holds 128 live particles. `dest_bin`: A permutation of the bins; every block stays on a device with the same gx and gy index, and each device sends at most 1 block to any one device, a bound that some pair of devices reaches.
All inputs are finite; a program needn't handle non-finite values.
Results may differ from a plain program's by a relative error of at most 0.0065.
The roundings to bfloat16 on the way count: a program that leaves them out, or rounds other values in their place, can miss the bound.
Values may be sent and summed in bfloat16 or wider, within the bound.
No kernel may reach another device: no remote copies, remote signals or barrier semaphores. Data moves between devices by JAX's collectives and lax.ppermute only.
A program may use at most 64 MiB of HBM per device.

v0:
```python
import math

import jax
import jax.numpy as jnp
import numpy as np
from jax import lax
from jax.experimental import pallas as pl
from jax.experimental.pallas import tpu as pltpu
from jax.sharding import PartitionSpec as P

HEADS = 8
EPSILON = 1e-05
LOG2E = 1.4426950408889634
DEAD = -1e30
HEAD_ROWS = 16
ROLES = 2
ENDS = ((None, 'ring'), (None, 'ring'))

F32 = jnp.float32
BF16 = jnp.bfloat16

VMEM = pl.BlockSpec(memory_space=pltpu.VMEM)
ROWS = (((1,), (1,)), ((), ()))
COLUMNS = (((0,), (1,)), ((), ()))
TURNED = (((0,), (0,)), ((), ()))


def shape(dims, dtype):
    return jax.ShapeDtypeStruct(dims, dtype)


def call(body, outs, specs, scratch=(), limit=30 << 20):
    return pl.pallas_call(
        body,
        out_shape=outs,
        in_specs=specs,
        out_specs=jax.tree.map(lambda _: VMEM, outs),
        scratch_shapes=scratch,
        compiler_params=pltpu.CompilerParams(vmem_limit_bytes=limit),
    )


def swaps(count, parity):
    pairs = []
    for low in range(parity, count - 1, 2):
        pairs += [(low, low + 1), (low + 1, low)]
    return pairs


def swap(block, axis, parity, ends):
    count = lax.axis_size(axis)
    pairs = swaps(count, parity)
    if parity == 1 and count % 2 == 0 and count > 2:
        if ends == "ring":
            pairs += [(0, count - 1), (count - 1, 0)]
        if ends == "peer" and lax.axis_size("gz") == 2:
            names = ("gx", "gy", "gz")
            sizes = [lax.axis_size(n) for n in names]
            grid = np.arange(math.prod(sizes)).reshape(sizes)
            along = np.moveaxis(grid, names.index(axis), 0)
            outer = along[[0, -1]]
            pairs = [
                (int(i), int(j)) for a, b in pairs for i, j in zip(along[a].flat, along[b].flat)
            ]
            pairs += [(int(i), int(j)) for i, j in zip(outer.flat, outer[..., ::-1].flat)]
            axis = names
    return lax.ppermute(block, axis, pairs)


def dot(a, b, dims=(((1,), (0,)), ((), ()))):
    return lax.dot_general(a, b, dims, preferred_element_type=F32)


def layer_norm(values, gain):
    centre = values - jnp.mean(values, axis=-1, keepdims=True)
    spread = jnp.mean(centre * centre, axis=-1, keepdims=True)
    return centre * lax.rsqrt(spread + EPSILON) * gain


def live_rows(block, slots, present=None):
    count = block[slots : slots + 1, :128].astype(F32)
    if present is not None:
        count = jnp.where(present, count, 0.0)
    row = lax.broadcasted_iota(jnp.int32, (slots, 128), 0).astype(F32)
    return jnp.where(row < count, 0.0, DEAD).astype(BF16)


def prepare_body(out):
    out[...] = jnp.zeros_like(out)


def prepare(slots, width):
    return pl.pallas_call(
        prepare_body,
        out_shape=shape((8, 128), F32),
        out_specs=VMEM,
        compiler_params=pltpu.CompilerParams(vmem_limit_bytes=1 << 20),
        cost_estimate=pl.CostEstimate(
            flops=80000 * slots * width, transcendentals=0, bytes_accessed=0
        ),
        name="prepare",
    )()


def entry(pair, index):
    return jnp.where(index == 0, pair[:, 0:1], pair[:, 1:2])


def scalar(block):
    return jnp.sum(block.astype(F32)).astype(jnp.int32)


def pack_body(features, counts, ready, both, first, second, residual):
    slots, width = features.shape[1:]
    parity = lax.axis_index("gy") % 2
    del ready
    for role, single in ((0, first), (1, second)):
        held = 1 - parity if role == 0 else parity
        state = features[held]
        residual[role] = state
        rows = state.astype(BF16)
        row = lax.broadcasted_iota(jnp.int32, (HEAD_ROWS, width), 0)
        top = jnp.where(row == 1, role, entry(counts[...], held)).astype(F32).astype(BF16)
        both[role, :slots] = rows
        both[role, slots:] = top
        single[:slots] = rows
        single[slots:] = top


def pack(features, counts, ready):
    bins, slots, width = features.shape
    tall = slots + HEAD_ROWS
    outs = [
        shape((bins, tall, width), BF16),
        shape((tall, width), BF16),
        shape((tall, width), BF16),
        shape((bins, slots, width), F32),
    ]
    return call(pack_body, outs, [VMEM] * 3)(
        features, counts.reshape(1, bins), ready
    )


def score_keys(keys, biases, width):
    bias = jnp.concatenate(biases, axis=0)
    return [
        jnp.concatenate([keys[:, at : at + 128], bias], axis=1) for at in range(0, width, 128)
    ]


def pick(array, places, slots, axis):
    parts = [lax.slice_in_dim(array, p * slots, (p + 1) * slots, axis=axis) for p in places]
    return jnp.concatenate(parts, axis=axis)


def scores_part(part, pair, per_group, mask, outs, at, factor):
    powers, peaks, sums = outs
    scores = dot(part[2 * pair // per_group], mask, ROWS)
    peak = jnp.max(scores, axis=0, keepdims=True)
    power = jnp.exp2((scores - peak) * factor)
    powers[at] = power
    peaks[at] = peak
    sums[at] = jnp.sum(power, axis=0, keepdims=True)


def constants(width):
    head_size = width // HEADS
    return head_size, HEADS * 128 // width, head_size ** (-0.5) * LOG2E


def early_body(own, near, weights, outs):
    query_weight, key_weight, value_weight = weights
    masks, turned_values, *parts = outs
    width = own.shape[-1]
    slots = own.shape[1] - HEAD_ROWS
    head_size, per_group, factor = constants(width)
    blocks = [own[0], own[1], *near]
    rows = jnp.concatenate([b[:slots] for b in blocks], axis=0)
    biases = [live_rows(b, slots) for b in blocks]
    queries = dot(rows[: ROLES * slots], query_weight[...]).astype(BF16)
    keys = dot(rows, key_weight[...]).astype(BF16)
    lane = lax.broadcasted_iota(jnp.int32, (slots, 128), 1)
    mark = jnp.where(lane == 0, 1.0, 0.0).astype(BF16)
    places = [[0, 1] + ([2 + role] if near else []) for role in range(ROLES)]
    for role in range(ROLES):
        part = score_keys(
            pick(keys, places[role], slots, 0), [biases[p] for p in places[role]], width
        )
        for pair in range(HEADS // 2):
            masked = []
            for head in (2 * pair, 2 * pair + 1):
                group, inner = divmod(head, per_group)
                query = queries[role * slots : (role + 1) * slots]
                query = query[:, group * 128 : (group + 1) * 128]
                inside = (lane >= inner * head_size) & (lane < (inner + 1) * head_size)
                query = jnp.where(inside, query.astype(F32), 0.0).astype(BF16)
                masked.append(jnp.concatenate([query, mark], axis=1))
            masked = jnp.concatenate(masked, axis=0)
            at = role * (HEADS // 2) + pair
            masks[at] = masked
            scores_part(part, pair, per_group, masked, parts, at, factor)
    values = dot(value_weight[...], rows, COLUMNS).astype(BF16)
    for role in range(ROLES):
        turned_values[role] = pick(values, places[role], slots, 1)


def part_shapes(slots, width, blocks):
    keys = blocks * slots
    pairs = ROLES * HEADS // 2
    return [
        shape((ROLES, width, keys), BF16),
        shape((pairs, keys, 2 * slots), F32),
        shape((pairs, 1, 2 * slots), F32),
        shape((pairs, 1, 2 * slots), F32),
    ]


def run_early(own, beside, weights):
    slots, width = own.shape[1] - HEAD_ROWS, own.shape[2]

    def body(own, *refs):
        near = []
        if beside:
            peer, left = refs[0][...], refs[1][...]
            role = peer[slots + 1 : slots + 2].astype(F32)
            near = [choose(role, peer, left).astype(BF16), choose(role, left, peer).astype(BF16)]
        n = len(beside)
        early_body(own, near, refs[n : n + 3], refs[n + 3 :])

    outs = part_shapes(slots, width, 3 if beside else 2)
    outs = [shape((ROLES * HEADS // 2, 2 * slots, 256), BF16)] + outs
    args = [own, *beside, *weights[:3]]
    masks, *part = call(body, outs, [VMEM] * len(args))(*args)
    return masks, part


def run_middle(far, masks, weights, around):
    slots, width = far[0][0].shape[1] - HEAD_ROWS, far[0][0].shape[2]
    n = len(far)
    _, per_group, factor = constants(width)

    def body(*refs):
        halos, (masks, key_weight, value_weight), outs = refs[:n], refs[n : n + 3], refs[n + 3 :]
        turned_values, *parts = outs
        blocks, biases = [], []
        for role in range(ROLES):
            for halo, (_, axis) in zip(halos, far):
                block = halo[role]
                blocks.append(block[:slots])
                biases.append(live_rows(block, slots, inside(axis, around)))
        rows = jnp.concatenate(blocks, axis=0)
        keys = dot(rows, key_weight[...]).astype(BF16)
        for role in range(ROLES):
            span = slice(role * n * slots, (role + 1) * n * slots)
            part = score_keys(keys[span], biases[role * n : (role + 1) * n], width)
            for pair in range(HEADS // 2):
                at = role * (HEADS // 2) + pair
                scores_part(part, pair, per_group, masks[at], parts, at, factor)
        values = dot(value_weight[...], rows, COLUMNS).astype(BF16)
        for role in range(ROLES):
            turned_values[role] = values[:, role * n * slots : (role + 1) * n * slots]

    args = [block for block, _ in far] + [masks, weights[1], weights[2]]
    return call(body, part_shapes(slots, width, n), [VMEM] * len(args))(*args)


def inside(axis, around):
    if axis is None or not around:
        return None
    index = lax.axis_index(axis)
    return (index > 0) & (index < lax.axis_size(axis) - 1)


def attend_role(role, block, flag, masks, parts, key_weight, value_weight):
    width = block.shape[1]
    slots = block.shape[0] - HEAD_ROWS
    head_size, per_group, factor = constants(width)
    rows = block[:slots]
    keys = score_keys(
        dot(rows, key_weight[...]).astype(BF16), [live_rows(block, slots, flag)], width
    )
    values = dot(value_weight[...], rows, COLUMNS).astype(BF16)
    pieces = []
    for pair in range(HEADS // 2):
        at = role * (HEADS // 2) + pair
        scores = dot(keys[2 * pair // per_group], masks[at], ROWS)
        peak = jnp.max(scores, axis=0, keepdims=True)
        for _, _, peaks, _ in parts:
            peak = jnp.maximum(peak, peaks[at])
        power = jnp.exp2((scores - peak) * factor)
        total = jnp.sum(power, axis=0, keepdims=True)
        rescales = []
        for _, _, peaks, sums in parts:
            rescales.append(jnp.exp2((peaks[at] - peak) * factor))
            total = total + sums[at] * rescales[-1]
        inverse = 1.0 / total
        feature = slice(2 * pair * head_size, 2 * (pair + 1) * head_size)
        mixed = dot(values[feature], (power * inverse).astype(BF16))
        for (turned, powers, _, _), rescale in zip(parts, rescales):
            weights = (powers[at] * (rescale * inverse)).astype(BF16)
            mixed = mixed + dot(turned[role, feature], weights)
        pieces += [mixed[:head_size, :slots], mixed[head_size:, slots:]]
    return jnp.concatenate(pieces, axis=0).astype(BF16)


def update(state, attended, out_weight, up_weight, down_weight, attention_gain, feed_gain):
    mixed = jnp.concatenate([dot(a, out_weight[...], TURNED) for a in attended], axis=0)
    hidden = layer_norm(state + mixed, attention_gain[...])
    inner = jax.nn.gelu(dot(hidden.astype(BF16), up_weight[...])).astype(BF16)
    return layer_norm(hidden + dot(inner, down_weight[...]), feed_gain[...])


def keep_live(result, top):
    row = lax.broadcasted_iota(jnp.int32, result.shape, 0).astype(F32)
    return jnp.where(row < top, result, 0.0)


def run_bins(residual, own, sides, around, masks, parts, weights, gains):
    bins, slots, width = residual.shape
    args = [residual, own, *sides, masks, *parts[0], *parts[1], *weights[1:], *gains]

    def body(residual, own, first, second, masks, *refs):
        parts, refs = (refs[:4], refs[4:8]), refs[8:]
        key_weight, value_weight, *rest, out = refs
        attended = [
            attend_role(role, side[...], flag, masks, parts, key_weight, value_weight)
            for role, side, flag in ((0, first, None), (1, second, inside("gy", around)))
        ]
        state = jnp.concatenate([residual[0], residual[1]], axis=0)
        result = update(state, attended, *rest)
        parity = lax.axis_index("gy") % 2
        for role in range(ROLES):
            rows = result[role * slots : (role + 1) * slots]
            rows = keep_live(rows, own[role, slots : slots + 1, :].astype(F32))
            out[1 - parity if role == 0 else parity] = rows

    outs = shape((bins, slots, width), F32)
    return call(body, outs, [VMEM] * len(args))(*args)


def run_one(leaving, spans, residual, own, sides, around, masks, parts, weights, gains, places):
    _, slots, width = residual.shape
    tall = slots + HEAD_ROWS
    args = [places, residual, own, *sides, masks, *parts[0], *parts[1], *weights[1:], *gains]

    def body(places, residual, own, first, second, masks, *refs):
        parts, refs = (refs[:4], refs[4:8]), refs[8:]
        key_weight, value_weight, *rest = refs[:7]
        outs = refs[7:]
        parity = lax.axis_index("gy") % 2
        stays = scalar(entry(places[...], 1 - parity)) % spans[1] == lax.axis_index("gz")
        role = jnp.where(stays, 1, 0) if leaving else jnp.where(stays, 0, 1)
        place = scalar(entry(places[...], jnp.where(role == 0, 1 - parity, parity)))
        new_role = jnp.where((place // spans[1]) % 2 == parity, 1, 0)
        ahead = role == 0
        block = jnp.where(ahead, first[...].astype(F32), second[...].astype(F32)).astype(BF16)
        flag = inside("gy", around)
        flag = flag if flag is None else ahead | flag
        attended = attend_role(role, block, flag, masks, parts, key_weight, value_weight)
        result = update(residual[role], [attended], *rest)
        top = own[role, slots:].astype(F32)
        result = keep_live(result, top[:1])
        line = lax.broadcasted_iota(jnp.int32, (HEAD_ROWS, width), 0)
        outs[0][:slots] = result.astype(BF16)
        outs[0][slots:] = jnp.where(line == 1, new_role.astype(F32), top).astype(BF16)
        if not leaving:
            outs[1][...] = result

    outs = [shape((tall, width), BF16)]
    if not leaving:
        outs.append(shape((slots, width), F32))
    args[0] = places.reshape(1, -1)
    return call(body, outs, [VMEM] * len(args))(*args)


def choose(role, yes, no):
    return jnp.where(role < 0.5, yes.astype(F32), no.astype(F32))


def settle_body(stay, stayed, came, both, first, second, residual):
    slots = stayed.shape[0]
    stay, came = stay[...], came[...]
    role = stay[slots + 1 : slots + 2].astype(F32)
    for index, single in ((0, first), (1, second)):
        block = choose(role, *((stay, came) if index == 0 else (came, stay))).astype(BF16)
        both[index] = block
        single[...] = block
        rows = stayed[...], came[:slots]
        residual[index] = choose(role, *(rows if index == 0 else rows[::-1]))


def settle(stay, stayed, came):
    slots, width = stayed.shape
    tall = slots + HEAD_ROWS
    outs = [
        shape((ROLES, tall, width), BF16),
        shape((tall, width), BF16),
        shape((tall, width), BF16),
        shape((ROLES, slots, width), F32),
    ]
    return call(settle_body, outs, [VMEM] * 3)(stay, stayed, came)


def relocate(state, counts, dest_bin, bins_y):
    total, slots, width = state.shape
    depth = lax.axis_size("gz")
    targets = dest_bin.reshape(-1)
    peer = targets % depth
    local = targets // depth % bins_y
    order = jnp.arange(total, dtype=jnp.int32)
    earlier = (peer[None, :] == peer[:, None]) & (order[None, :] < order[:, None])
    slot = jnp.sum(earlier.astype(jnp.int32), axis=1)
    capacity = (total + depth - 1) // depth
    outgoing = jnp.zeros((depth, capacity, slots, width), F32).at[peer, slot].set(state)
    outgoing_counts = jnp.zeros((depth, capacity), jnp.int32).at[peer, slot].set(counts)
    outgoing_places = jnp.full((depth, capacity), total, jnp.int32).at[peer, slot].set(local)
    arrived = lax.all_to_all(outgoing.astype(BF16), "gz", 0, 0, tiled=True).astype(F32)
    arrived_counts = lax.all_to_all(outgoing_counts, "gz", 0, 0, tiled=True)
    places = lax.all_to_all(outgoing_places, "gz", 0, 0, tiled=True).reshape(-1)
    moved = jnp.zeros((total, slots, width), F32)
    moved = moved.at[places].set(arrived.reshape(-1, slots, width), mode="drop")
    moved_counts = jnp.zeros((total,), jnp.int32)
    moved_counts = moved_counts.at[places].set(arrived_counts.reshape(-1), mode="drop")
    return moved, moved_counts


def exchange(own, first, second, axes, ends):
    far = []
    for axis in axes:
        for parity in range(2):
            if not swaps(lax.axis_size(axis), parity):
                continue
            how = ends[0] if axis == "gx" else None
            block = swap(own, axis, parity, how)
            far.append((block, axis if how and parity == 1 else None))
    sides = []
    for parity, block in ((0, first), (1, second)):
        sides.append(swap(block, "gy", parity, ends[1]))
    return far, sides


def shards(features, occupancy, dest_bin, *rest):
    weights, gains = rest[:6], [g.reshape(1, -1) for g in rest[6:]]
    slots, width = features.shape[3:]
    state = features.reshape(2, slots, width)
    counts = occupancy.reshape(2)
    places = dest_bin.reshape(2)
    depth = lax.axis_size("gz")
    spans = (2 * lax.axis_size("gy"), depth)

    def finish(own, residual, beside, far, sides, ends):
        around = bool(ends[1])
        masks, first = run_early(own, beside, weights)
        second = run_middle(far, masks, weights, True)
        return residual, own, sides, around, masks, (first, second), weights, gains

    ready = prepare(slots, width)
    own, first, second, residual = pack(state, counts, ready)
    far, sides = exchange(own, first, second, ("gx", "gz"), ENDS[0])
    known = finish(own, residual, [], far, sides, ENDS[0])
    if depth == 2:
        (leave,) = run_one(True, spans, *known, places)
        came = swap(leave, "gz", 0, None)
        stay, stayed = run_one(False, spans, *known, places)
        peer = swap(stay, "gz", 0, None)
        own, first, second, residual = settle(stay, stayed, came)
        beside, axes = [peer, leave], ("gx",)
    else:
        state = run_bins(*known)
    if depth != 2:
        state, counts = relocate(state, counts, places, 2)
        own, first, second, residual = pack(state, counts, ready)
        beside, axes = [], ("gx", "gz")
    far, sides = exchange(own, first, second, axes, ENDS[1])
    out = run_bins(*finish(own, residual, beside, far, sides, ENDS[1]))
    return out.reshape(features.shape)


def solution(mesh):
    placed = (
        P("gx", "gy", "gz", None, None),
        P("gx", "gy", "gz"),
        P("gx", "gy", "gz"),
        *([P()] * 8),
    )
    return jax.shard_map(
        shards,
        mesh=mesh,
        in_specs=placed,
        out_specs=P("gx", "gy", "gz", None, None),
        check_vma=False,
    )
```

profile of v0, /device:TPU:0, one launch (start us, length us, event | category | flops | bytes accessed | tf_op | source)
XLA Modules:
  0.0 35.3 jit_solution(9048945420898652708)
XLA Ops:
  0.0 0.0 copy-start.10
  0.0 0.0 copy-start.6
  0.0 0.0 copy-start.1
  0.0 0.0 copy-start
  0.0 0.0 copy-start.5
  0.0 0.0 copy-start.3
  0.0 0.0 copy-start.2
  0.0 0.0 copy-start.4
  0.0 0.0 copy-start.8
  0.1 0.0 copy-start.7
  0.1 0.0 copy-start.9
  0.1 0.6 %copy-done.10 = s32[1,2,1]{1,2,0:T(1,128)S(1)} copy-done((s32[1,2,1]{1,2,0:T(1,128)S(1)}, s32[1,2,1]{1,2,0:T(1,128)}, u32[]{:S(2)}) %copy-start.10) | copy-done | bytes 32
  0.7 0.3 copy-done.6
  1.0 0.1 shard_map.109
  1.1 3.0 %collective-permute-start.4 = (bf16[2,144,256]{2,1,0:T(8,128)(2,1)S(1)}, bf16[2,144,256]{2,1,0:T(8,128)(2,1)S(1)}, u32[]{:S(2)}, u32[]{:S(2)}) collective-permute-start(bf16[2,144,256]{2,1,0:T(8,128)(2,1)S(1)} %get-tuple-element.34.own), channel_id=1, source_target_pairs={{0,1},{1,0},{2,3},{3,2},{4,5},{5,4},{6,7},{7,6},{8,9},{9,8},{10,11... | collective-permute-start | bytes 442376 | tf_op jit(solution)/shard_map/ppermute | solution.py:67
  4.1 0.7 %collective-permute-start.3 = (bf16[2,144,256]{2,1,0:T(8,128)(2,1)S(1)}, bf16[2,144,256]{2,1,0:T(8,128)(2,1)S(1)}, u32[]{:S(2)}, u32[]{:S(2)}) collective-permute-start(bf16[2,144,256]{2,1,0:T(8,128)(2,1)S(1)} %get-tuple-element.34.own), channel_id=1, source_target_pairs={{8,16},{16,8},{9,17},{17,9},{10,18},{18,10},{11,19},{19,11},{12,20... | collective-permute-start | bytes 442376 | tf_op jit(solution)/shard_map/ppermute | solution.py:67
  4.8 4.5 %collective-permute-start.2 = (bf16[2,144,256]{2,1,0:T(8,128)(2,1)S(1)}, bf16[2,144,256]{2,1,0:T(8,128)(2,1)S(1)}, u32[]{:S(2)}, u32[]{:S(2)}) collective-permute-start(bf16[2,144,256]{2,1,0:T(8,128)(2,1)S(1)} %get-tuple-element.34.own), channel_id=1, source_target_pairs={{0,8},{8,0},{16,24},{24,16},{1,9},{9,1},{17,25},{25,17},{2,10},{10... | collective-permute-start | bytes 442376 | tf_op jit(solution)/shard_map/ppermute | solution.py:67
  9.2 0.0 collective-permute-start
  9.2 1.6 %collective-permute-start.1 = (bf16[144,256]{1,0:T(8,128)(2,1)S(1)}, bf16[144,256]{1,0:T(8,128)(2,1)S(1)}, u32[]{:S(2)}, u32[]{:S(2)}) collective-permute-start(bf16[144,256]{1,0:T(8,128)(2,1)S(1)} %get-tuple-element.36), channel_id=1, source_target_pairs={{2,4},{4,2},{0,6},{6,0},{3,5},{5,3},{1,7},{7,1},{10,12},{12,10},{8... | collective-permute-start | bytes 221192 | tf_op jit(solution)/shard_map/ppermute | solution.py:67
  10.8 0.0 copy-done.1
  10.8 0.0 copy-done
  10.8 0.0 copy-done.5
  10.8 1.0 %shard_map.110 = (bf16[8,256,256]{2,1,0:T(8,128)(2,1)S(1)}, bf16[2,256,256]{2,1,0:T(8,128)(2,1)S(1)}, f32[8,256,256]{2,1,0:T(8,128)S(1)}, f32[8,1,256]{2,1,0:T(1,128)S(1)}, f32[8,1,256]{2,1,0:T(1,128)S(1)}) custom-call(bf16[2,144,256]{2,1,0:T(8,128)(2,1)S(1)} %get-tuple-element.34.own, bf16[256,256]{1,0:T(8,128)(2,1)S(1)} %copy-done.5, ...), custom_call_target="tpu_custom_call" | custom-call | tf_op jit(solution)/shard_map/pallas_call | solution.py:233
  11.8 0.0 collective-permute-done.4.refs_2_
  11.8 0.0 collective-permute-done.3.refs_1_
  11.8 0.7 %collective-permute-done.2.refs_0_ = bf16[2,144,256]{2,1,0:T(8,128)(2,1)S(1)} collective-permute-done((bf16[2,144,256]{2,1,0:T(8,128)(2,1)S(1)}, bf16[2,144,256]{2,1,0:T(8,128)(2,1)S(1)}, u32[]{:S(2)}, u32[]{:S(2)}) %collective-permute-start.2) | collective-permute-done | bytes 147488 | tf_op jit(solution)/shard_map/ppermute | solution.py:67
  12.5 1.2 %shard_map.111 = (bf16[2,256,384]{2,1,0:T(8,128)(2,1)S(1)}, f32[8,384,256]{2,1,0:T(8,128)S(1)}, f32[8,1,256]{2,1,0:T(1,128)S(1)}, f32[8,1,256]{2,1,0:T(1,128)S(1)}) custom-call(bf16[2,144,256]{2,1,0:T(8,128)(2,1)S(1)} %collective-permute-done.2.refs_0_, bf16[2,144,256]{2,1,0:T(8,128)(2,1)S(1)} %collective-permute-done.3.refs_1_, ...), custom_call_target="tpu_custom_call" | custom-call | tf_op jit(solution)/shard_map/pallas_call | solution.py:264
  13.7 0.0 collective-permute-done.first
  13.7 0.0 collective-permute-done.1.second
  13.7 0.0 copy-done.3
  13.8 0.0 copy-done.2
  13.8 0.0 copy-done.4
  13.8 0.0 copy-done.8
  13.8 0.0 copy-done.7
  13.8 0.0 copy-done.9
  13.8 2.1 %shard_map.113.refs_1_ = bf16[144,256]{1,0:T(8,128)(2,1)S(1)} custom-call(s32[1,2]{1,0:T(1,128)S(1)} %bitcast.15, f32[2,128,256]{2,1,0:T(8,128)S(1)} %get-tuple-element.33.residual, bf16[2,144,256]{2,1,0:T(8,128)(2,1)S(1)} %get-tuple-element.34.own, bf16[144,256]{1,0:T(8,128)(2,1)S(1)} %collective-permute-done.first, ...), custom_call_target="tpu_custom_call" | custom-call | tf_op jit(solution)/shard_map/pallas_call | solution.py:373
  15.9 0.6 %collective-permute-start.5 = (bf16[144,256]{1,0:T(8,128)(2,1)S(1)}, bf16[144,256]{1,0:T(8,128)(2,1)S(1)}, u32[]{:S(2)}, u32[]{:S(2)}) collective-permute-start(bf16[144,256]{1,0:T(8,128)(2,1)S(1)} %shard_map.113.refs_1_), channel_id=1, source_target_pairs={{0,1},{1,0},{2,3},{3,2},{4,5},{5,4},{6,7},{7,6},{8,9},{9,8},{10,11... | collective-permute-start | bytes 221192 | tf_op jit(solution)/shard_map/ppermute | solution.py:67
  16.5 2.1 %shard_map.112 = (bf16[144,256]{1,0:T(8,128)(2,1)S(1)}, f32[128,256]{1,0:T(8,128)S(1)}) custom-call(s32[1,2]{1,0:T(1,128)S(1)} %bitcast.16, f32[2,128,256]{2,1,0:T(8,128)S(1)} %get-tuple-element.33.residual, bf16[2,144,256]{2,1,0:T(8,128)(2,1)S(1)} %get-tuple-element.34.own, bf16[144,256]{1,0:T(8,128)(2,1)S(1)} %collective-permute-done.first, ...), custom_call_target="tpu_custom_call" | custom-call | tf_op jit(solution)/shard_map/pallas_call | solution.py:373
  18.6 1.7 %collective-permute-done.5.came = bf16[144,256]{1,0:T(8,128)(2,1)S(1)} collective-permute-done((bf16[144,256]{1,0:T(8,128)(2,1)S(1)}, bf16[144,256]{1,0:T(8,128)(2,1)S(1)}, u32[]{:S(2)}, u32[]{:S(2)}) %collective-permute-start.5) | collective-permute-done | bytes 73760 | tf_op jit(solution)/shard_map/ppermute | solution.py:67
  20.3 0.1 shard_map.114
  20.4 0.7 %collective-permute-start.10 = (bf16[2,144,256]{2,1,0:T(8,128)(2,1)S(1)}, bf16[2,144,256]{2,1,0:T(8,128)(2,1)S(1)}, u32[]{:S(2)}, u32[]{:S(2)}) collective-permute-start(bf16[2,144,256]{2,1,0:T(8,128)(2,1)S(1)} %get-tuple-element.49.own), channel_id=1, source_target_pairs={{8,16},{16,8},{9,17},{17,9},{10,18},{18,10},{11,19},{19,11},{12,20... | collective-permute-start | bytes 442376 | tf_op jit(solution)/shard_map/ppermute | solution.py:67
  21.1 3.6 %collective-permute-start.9 = (bf16[2,144,256]{2,1,0:T(8,128)(2,1)S(1)}, bf16[2,144,256]{2,1,0:T(8,128)(2,1)S(1)}, u32[]{:S(2)}, u32[]{:S(2)}) collective-permute-start(bf16[2,144,256]{2,1,0:T(8,128)(2,1)S(1)} %get-tuple-element.49.own), channel_id=1, source_target_pairs={{0,8},{8,0},{16,24},{24,16},{1,9},{9,1},{17,25},{25,17},{2,10},{10... | collective-permute-start | bytes 442376 | tf_op jit(solution)/shard_map/ppermute | solution.py:67
  24.7 0.5 %collective-permute-start.8 = (bf16[144,256]{1,0:T(8,128)(2,1)S(1)}, bf16[144,256]{1,0:T(8,128)(2,1)S(1)}, u32[]{:S(2)}, u32[]{:S(2)}) collective-permute-start(bf16[144,256]{1,0:T(8,128)(2,1)S(1)} %get-tuple-element.46.stay), channel_id=1, source_target_pairs={{0,1},{1,0},{2,3},{3,2},{4,5},{5,4},{6,7},{7,6},{8,9},{9,8},{10,11... | collective-permute-start | bytes 221192 | tf_op jit(solution)/shard_map/ppermute | solution.py:67
  25.2 0.0 collective-permute-start.6
  25.2 1.6 %collective-permute-start.7 = (bf16[144,256]{1,0:T(8,128)(2,1)S(1)}, bf16[144,256]{1,0:T(8,128)(2,1)S(1)}, u32[]{:S(2)}, u32[]{:S(2)}) collective-permute-start(bf16[144,256]{1,0:T(8,128)(2,1)S(1)} %get-tuple-element.51), channel_id=1, source_target_pairs={{2,4},{4,2},{0,6},{6,0},{3,5},{5,3},{1,7},{7,1},{10,12},{12,10},{8... | collective-permute-start | bytes 221192 | tf_op jit(solution)/shard_map/ppermute | solution.py:67
  26.8 2.2 %collective-permute-done.8.refs_0_ = bf16[144,256]{1,0:T(8,128)(2,1)S(1)} collective-permute-done((bf16[144,256]{1,0:T(8,128)(2,1)S(1)}, bf16[144,256]{1,0:T(8,128)(2,1)S(1)}, u32[]{:S(2)}, u32[]{:S(2)}) %collective-permute-start.8) | collective-permute-done | bytes 73760 | tf_op jit(solution)/shard_map/ppermute | solution.py:67
  29.0 1.3 %shard_map.115 = (bf16[8,256,256]{2,1,0:T(8,128)(2,1)S(1)}, bf16[2,256,384]{2,1,0:T(8,128)(2,1)S(1)}, f32[8,384,256]{2,1,0:T(8,128)S(1)}, f32[8,1,256]{2,1,0:T(1,128)S(1)}, f32[8,1,256]{2,1,0:T(1,128)S(1)}) custom-call(bf16[2,144,256]{2,1,0:T(8,128)(2,1)S(1)} %get-tuple-element.49.own, bf16[144,256]{1,0:T(8,128)(2,1)S(1)} %collective-permute-done.8.refs_0_, ...), custom_call_target="tpu_custom_call" | custom-call | tf_op jit(solution)/shard_map/pallas_call | solution.py:233
  30.4 0.0 collective-permute-done.10.refs_1_
  30.4 0.0 collective-permute-done.9.refs_0_
  30.4 0.9 %shard_map.116 = (bf16[2,256,256]{2,1,0:T(8,128)(2,1)S(1)}, f32[8,256,256]{2,1,0:T(8,128)S(1)}, f32[8,1,256]{2,1,0:T(1,128)S(1)}, f32[8,1,256]{2,1,0:T(1,128)S(1)}) custom-call(bf16[2,144,256]{2,1,0:T(8,128)(2,1)S(1)} %collective-permute-done.9.refs_0_, bf16[2,144,256]{2,1,0:T(8,128)(2,1)S(1)} %collective-permute-done.10.refs_1_, ...), custom_call_target="tpu_custom_call" | custom-call | tf_op jit(solution)/shard_map/pallas_call | solution.py:264
  31.3 0.0 collective-permute-done.6.first
  31.3 0.0 collective-permute-done.7.second
  31.3 4.0 %shard_map.117 = f32[2,128,256]{2,1,0:T(8,128)} custom-call(f32[2,128,256]{2,1,0:T(8,128)S(1)} %get-tuple-element.48.residual, bf16[2,144,256]{2,1,0:T(8,128)(2,1)S(1)} %get-tuple-element.49.own, bf16[144,256]{1,0:T(8,128)(2,1)S(1)} %collective-permute-done.6.first, bf16[144,256]{1,0:T(8,128)(2,1)S(1)} %collective-permute-done.7.second, ...), custom_call_target="tpu_custom_call" | custom-call | tf_op jit(solution)/shard_map/pallas_call | solution.py:338
  (1 shorter events, 0.0 us)
Async XLA Ops:
  0.0 0.7 %copy-start.10 = (s32[1,2,1]{1,2,0:T(1,128)S(1)}, s32[1,2,1]{1,2,0:T(1,128)}, u32[]{:S(2)}) copy-start(s32[1,2,1]{1,2,0:T(1,128)} %param.12) | copy-start | bytes 28
  0.0 1.0 %copy-start.6 = (f32[1,2,1,128,256]{4,3,2,1,0:T(8,128)S(1)}, f32[1,2,1,128,256]{4,3,2,1,0:T(8,128)}, u32[]{:S(2)}) copy-start(f32[1,2,1,128,256]{4,3,2,1,0:T(8,128)} %param.11) | copy-start | bytes 786436
  0.0 10.8 %copy-start.1 = (bf16[256,256]{1,0:T(8,128)(2,1)S(1)}, bf16[256,256]{1,0:T(8,128)(2,1)}, u32[]{:S(2)}) copy-start(bf16[256,256]{1,0:T(8,128)(2,1)} %refs_9_.5) | copy-start | bytes 393220
  0.0 10.8 %copy-start = (bf16[256,256]{1,0:T(8,128)(2,1)S(1)}, bf16[256,256]{1,0:T(8,128)(2,1)}, u32[]{:S(2)}) copy-start(bf16[256,256]{1,0:T(8,128)(2,1)} %refs_8_.5) | copy-start | bytes 393220
  0.0 10.8 %copy-start.5 = (bf16[256,256]{1,0:T(8,128)(2,1)S(1)}, bf16[256,256]{1,0:T(8,128)(2,1)}, u32[]{:S(2)}) copy-start(bf16[256,256]{1,0:T(8,128)(2,1)} %refs_2_.3) | copy-start | bytes 393220
  0.0 13.7 %copy-start.3 = (bf16[1024,256]{1,0:T(8,128)(2,1)S(1)}, bf16[1024,256]{1,0:T(8,128)(2,1)}, u32[]{:S(2)}) copy-start(bf16[1024,256]{1,0:T(8,128)(2,1)} %refs_12_.5) | copy-start | bytes 1572868
  0.0 13.7 %copy-start.2 = (bf16[256,1024]{1,0:T(8,128)(2,1)S(1)}, bf16[256,1024]{1,0:T(8,128)(2,1)}, u32[]{:S(2)}) copy-start(bf16[256,1024]{1,0:T(8,128)(2,1)} %refs_11_.5) | copy-start | bytes 1572868
  0.0 13.7 %copy-start.4 = (bf16[256,256]{1,0:T(8,128)(2,1)S(1)}, bf16[256,256]{1,0:T(8,128)(2,1)}, u32[]{:S(2)}) copy-start(bf16[256,256]{1,0:T(8,128)(2,1)} %refs_10_.5) | copy-start | bytes 393220
  0.0 13.7 %copy-start.8 = (f32[256]{0:T(256)S(1)}, f32[256]{0:T(256)}, u32[]{:S(2)}) copy-start(f32[256]{0:T(256)} %param.21) | copy-start | bytes 3076
  0.1 13.7 %copy-start.7 = (f32[256]{0:T(256)S(1)}, f32[256]{0:T(256)}, u32[]{:S(2)}) copy-start(f32[256]{0:T(256)} %param.20) | copy-start | bytes 3076
  0.1 13.7 %copy-start.9 = (s32[1,2,1]{1,2,0:T(1,128)S(1)}, s32[1,2,1]{1,2,0:T(1,128)}, u32[]{:S(2)}) copy-start(s32[1,2,1]{1,2,0:T(1,128)} %param.13) | copy-start | bytes 28
  1.1 10.7 %collective-permute-start.4 = (bf16[2,144,256]{2,1,0:T(8,128)(2,1)S(1)}, bf16[2,144,256]{2,1,0:T(8,128)(2,1)S(1)}, u32[]{:S(2)}, u32[]{:S(2)}) collective-permute-start(bf16[2,144,256]{2,1,0:T(8,128)(2,1)S(1)} %get-tuple-element.34.own), channel_id=1, source_target_pairs={{0,1},{1,0},{2,3},{3,2},{4,5},{5,4},{6,7},{7,6},{8,9},{9,8},{10,11... | collective-permute-start | bytes 442376 | tf_op jit(solution)/shard_map/ppermute | solution.py:67
  4.1 7.7 %collective-permute-start.3 = (bf16[2,144,256]{2,1,0:T(8,128)(2,1)S(1)}, bf16[2,144,256]{2,1,0:T(8,128)(2,1)S(1)}, u32[]{:S(2)}, u32[]{:S(2)}) collective-permute-start(bf16[2,144,256]{2,1,0:T(8,128)(2,1)S(1)} %get-tuple-element.34.own), channel_id=1, source_target_pairs={{8,16},{16,8},{9,17},{17,9},{10,18},{18,10},{11,19},{19,11},{12,20... | collective-permute-start | bytes 442376 | tf_op jit(solution)/shard_map/ppermute | solution.py:67
  4.8 7.7 %collective-permute-start.2 = (bf16[2,144,256]{2,1,0:T(8,128)(2,1)S(1)}, bf16[2,144,256]{2,1,0:T(8,128)(2,1)S(1)}, u32[]{:S(2)}, u32[]{:S(2)}) collective-permute-start(bf16[2,144,256]{2,1,0:T(8,128)(2,1)S(1)} %get-tuple-element.34.own), channel_id=1, source_target_pairs={{0,8},{8,0},{16,24},{24,16},{1,9},{9,1},{17,25},{25,17},{2,10},{10... | collective-permute-start | bytes 442376 | tf_op jit(solution)/shard_map/ppermute | solution.py:67
  9.2 4.5 %collective-permute-start = (bf16[144,256]{1,0:T(8,128)(2,1)S(1)}, bf16[144,256]{1,0:T(8,128)(2,1)S(1)}, u32[]{:S(2)}, u32[]{:S(2)}) collective-permute-start(bf16[144,256]{1,0:T(8,128)(2,1)S(1)} %get-tuple-element.35), channel_id=1, source_target_pairs={{0,2},{2,0},{4,6},{6,4},{1,3},{3,1},{5,7},{7,5},{8,10},{10,8},{12,... | collective-permute-start | bytes 221192 | tf_op jit(solution)/shard_map/ppermute | solution.py:67
  9.2 4.5 %collective-permute-start.1 = (bf16[144,256]{1,0:T(8,128)(2,1)S(1)}, bf16[144,256]{1,0:T(8,128)(2,1)S(1)}, u32[]{:S(2)}, u32[]{:S(2)}) collective-permute-start(bf16[144,256]{1,0:T(8,128)(2,1)S(1)} %get-tuple-element.36), channel_id=1, source_target_pairs={{2,4},{4,2},{0,6},{6,0},{3,5},{5,3},{1,7},{7,1},{10,12},{12,10},{8... | collective-permute-start | bytes 221192 | tf_op jit(solution)/shard_map/ppermute | solution.py:67
  15.9 4.4 %collective-permute-start.5 = (bf16[144,256]{1,0:T(8,128)(2,1)S(1)}, bf16[144,256]{1,0:T(8,128)(2,1)S(1)}, u32[]{:S(2)}, u32[]{:S(2)}) collective-permute-start(bf16[144,256]{1,0:T(8,128)(2,1)S(1)} %shard_map.113.refs_1_), channel_id=1, source_target_pairs={{0,1},{1,0},{2,3},{3,2},{4,5},{5,4},{6,7},{7,6},{8,9},{9,8},{10,11... | collective-permute-start | bytes 221192 | tf_op jit(solution)/shard_map/ppermute | solution.py:67
  20.4 10.0 %collective-permute-start.10 = (bf16[2,144,256]{2,1,0:T(8,128)(2,1)S(1)}, bf16[2,144,256]{2,1,0:T(8,128)(2,1)S(1)}, u32[]{:S(2)}, u32[]{:S(2)}) collective-permute-start(bf16[2,144,256]{2,1,0:T(8,128)(2,1)S(1)} %get-tuple-element.49.own), channel_id=1, source_target_pairs={{8,16},{16,8},{9,17},{17,9},{10,18},{18,10},{11,19},{19,11},{12,20... | collective-permute-start | bytes 442376 | tf_op jit(solution)/shard_map/ppermute | solution.py:67
  21.1 9.3 %collective-permute-start.9 = (bf16[2,144,256]{2,1,0:T(8,128)(2,1)S(1)}, bf16[2,144,256]{2,1,0:T(8,128)(2,1)S(1)}, u32[]{:S(2)}, u32[]{:S(2)}) collective-permute-start(bf16[2,144,256]{2,1,0:T(8,128)(2,1)S(1)} %get-tuple-element.49.own), channel_id=1, source_target_pairs={{0,8},{8,0},{16,24},{24,16},{1,9},{9,1},{17,25},{25,17},{2,10},{10... | collective-permute-start | bytes 442376 | tf_op jit(solution)/shard_map/ppermute | solution.py:67
  24.7 4.4 %collective-permute-start.8 = (bf16[144,256]{1,0:T(8,128)(2,1)S(1)}, bf16[144,256]{1,0:T(8,128)(2,1)S(1)}, u32[]{:S(2)}, u32[]{:S(2)}) collective-permute-start(bf16[144,256]{1,0:T(8,128)(2,1)S(1)} %get-tuple-element.46.stay), channel_id=1, source_target_pairs={{0,1},{1,0},{2,3},{3,2},{4,5},{5,4},{6,7},{7,6},{8,9},{9,8},{10,11... | collective-permute-start | bytes 221192 | tf_op jit(solution)/shard_map/ppermute | solution.py:67
  25.2 6.1 %collective-permute-start.6 = (bf16[144,256]{1,0:T(8,128)(2,1)S(1)}, bf16[144,256]{1,0:T(8,128)(2,1)S(1)}, u32[]{:S(2)}, u32[]{:S(2)}) collective-permute-start(bf16[144,256]{1,0:T(8,128)(2,1)S(1)} %get-tuple-element.50), channel_id=1, source_target_pairs={{0,2},{2,0},{4,6},{6,4},{1,3},{3,1},{5,7},{7,5},{8,10},{10,8},{12,... | collective-permute-start | bytes 221192 | tf_op jit(solution)/shard_map/ppermute | solution.py:67
  25.2 6.1 %collective-permute-start.7 = (bf16[144,256]{1,0:T(8,128)(2,1)S(1)}, bf16[144,256]{1,0:T(8,128)(2,1)S(1)}, u32[]{:S(2)}, u32[]{:S(2)}) collective-permute-start(bf16[144,256]{1,0:T(8,128)(2,1)S(1)} %get-tuple-element.51), channel_id=1, source_target_pairs={{2,4},{4,2},{0,6},{6,0},{3,5},{5,3},{1,7},{7,1},{10,12},{12,10},{8... | collective-permute-start | bytes 221192 | tf_op jit(solution)/shard_map/ppermute | solution.py:67
where the time goes:
time: 35.4 us; the launch traced here: 35.3 us
  starting transfers between devices  16.7 us (47%)
  Pallas kernels  12.8 us (36%)
  waiting for transfers between devices  4.68 us (13%)
  local copies, waits for them, and re-layouts  0.92 us (3%)
    ppermute x11, starting transfers between devices, swap(): return lax.ppermute(block, axis, pairs)  16.7 us
    ppermute x11, waiting for transfers between devices, swap(): return lax.ppermute(block, axis, pairs)  4.68 us
    pallas_call x2, Pallas kernels, run_one(): return call(body, outs, [VMEM] * len(args))(*args)  4.21 us
    pallas_call x1, Pallas kernels, run_bins(): return call(body, outs, [VMEM] * len(args))(*args)  3.97 us
    pallas_call x2, Pallas kernels, run_early(): masks, *part = call(body, outs, [VMEM] * len(args))(*args)  2.3 us
    pallas_call x2, Pallas kernels, run_middle(): return call(body, part_shapes(slots, width, n), [VMEM] * len(args))(*args)  2.08 us
    unnamed x22, local copies, waits for them, and re-layouts  0.92 us
  transfers between devices with their start and end apart: 11, of which 3 were waited for; matrix products, arithmetic and copies ran while one was open for 0% of the time, Pallas kernels for 18%

commit v1 on v0

--- a/solution.py
+++ b/solution.py
@@ -14,6 +14,9 @@
 DEAD = -1e30
 HEAD_ROWS = 16
 ROLES = 2
+X0, X1, Y0, Y1, Z0, Z1 = [(axis, parity) for axis in ("gx", "gy", "gz") for parity in (0, 1)]
+ORDERS = ((X0, X1, Z0, Z1, Y0, Y1), (X0, X1, Z0, Z1, Y0, Y1))
+LAST = ((X1, Z0, Z1), (X1,))
 ENDS = ((None, 'ring'), (None, 'ring'))
 
 F32 = jnp.float32
@@ -29,12 +32,12 @@
     return jax.ShapeDtypeStruct(dims, dtype)
 
 
-def call(body, outs, specs, scratch=(), limit=30 << 20):
+def call(body, outs, specs, scratch=(), out_specs=None, limit=30 << 20):
     return pl.pallas_call(
         body,
         out_shape=outs,
         in_specs=specs,
-        out_specs=jax.tree.map(lambda _: VMEM, outs),
+        out_specs=out_specs or jax.tree.map(lambda _: VMEM, outs),
         scratch_shapes=scratch,
         compiler_params=pltpu.CompilerParams(vmem_limit_bytes=limit),
     )
@@ -271,19 +274,21 @@
     return (index > 0) & (index < lax.axis_size(axis) - 1)
 
 
-def attend_role(role, block, flag, masks, parts, key_weight, value_weight):
-    width = block.shape[1]
-    slots = block.shape[0] - HEAD_ROWS
+def attend_role(role, near, masks, parts, key_weight, value_weight, scratch):
+    side_keys, side_values, turned = scratch
+    width = near[0][0].shape[1]
+    slots = near[0][0].shape[0] - HEAD_ROWS
     head_size, per_group, factor = constants(width)
-    rows = block[:slots]
-    keys = score_keys(
-        dot(rows, key_weight[...]).astype(BF16), [live_rows(block, slots, flag)], width
-    )
-    values = dot(value_weight[...], rows, COLUMNS).astype(BF16)
-    pieces = []
-    for pair in range(HEADS // 2):
+    rows = jnp.concatenate([block[:slots] for block, _ in near], axis=0)
+    biases = [live_rows(block, slots, flag) for block, flag in near]
+    keys = score_keys(dot(rows, key_weight[...]).astype(BF16), biases, width)
+    for group, key in enumerate(keys):
+        side_keys[group] = key
+    side_values[...] = dot(value_weight[...], rows, COLUMNS).astype(BF16)
+
+    def step(pair):
         at = role * (HEADS // 2) + pair
-        scores = dot(keys[2 * pair // per_group], masks[at], ROWS)
+        scores = dot(side_keys[2 * pair // per_group], masks[at], ROWS)
         peak = jnp.max(scores, axis=0, keepdims=True)
         for _, _, peaks, _ in parts:
             peak = jnp.maximum(peak, peaks[at])
@@ -294,20 +299,40 @@
             rescales.append(jnp.exp2((peaks[at] - peak) * factor))
             total = total + sums[at] * rescales[-1]
         inverse = 1.0 / total
-        feature = slice(2 * pair * head_size, 2 * (pair + 1) * head_size)
-        mixed = dot(values[feature], (power * inverse).astype(BF16))
-        for (turned, powers, _, _), rescale in zip(parts, rescales):
+        feature = pl.ds(pl.multiple_of(2 * pair * head_size, 2 * head_size), 2 * head_size)
+        mixed = dot(side_values[feature], (power * inverse).astype(BF16))
+        for (turned_part, powers, _, _), rescale in zip(parts, rescales):
             weights = (powers[at] * (rescale * inverse)).astype(BF16)
-            mixed = mixed + dot(turned[role, feature], weights)
-        pieces += [mixed[:head_size, :slots], mixed[head_size:, slots:]]
-    return jnp.concatenate(pieces, axis=0).astype(BF16)
-
-
-def update(state, attended, out_weight, up_weight, down_weight, attention_gain, feed_gain):
-    mixed = jnp.concatenate([dot(a, out_weight[...], TURNED) for a in attended], axis=0)
+            mixed = mixed + dot(turned_part[role, feature], weights)
+        pieces = [mixed[:head_size, :slots], mixed[head_size:, slots:]]
+        turned[feature] = jnp.concatenate(pieces, axis=0).astype(BF16)
+
+    for pair in range(HEADS // 2):
+        step(pair)
+    return turned[...]
+
+
+def gelu(x):
+    half = 0.5 * x
+    return half + half * jnp.tanh(x * (0.7978845608028654 + 0.035677408136300125 * (x * x)))
+
+
+def update(state, attended, weights, gains):
+    out_weight, up_weight, down_weight = weights
+    attention_gain, feed_gain = gains
+    mixed = dot(attended, out_weight[...], TURNED)
     hidden = layer_norm(state + mixed, attention_gain[...])
-    inner = jax.nn.gelu(dot(hidden.astype(BF16), up_weight[...])).astype(BF16)
+    narrow = hidden.astype(BF16)
+    inner = gelu(dot(narrow, up_weight[...])).astype(BF16)
     return layer_norm(hidden + dot(inner, down_weight[...]), feed_gain[...])
+
+
+def late_scratch(slots, width, blocks):
+    return [
+        pltpu.VMEM((width // 128, blocks * slots, 256), BF16),
+        pltpu.VMEM((width, blocks * slots), BF16),
+        pltpu.VMEM((width, slots), BF16),
+    ]
 
 
 def keep_live(result, top):
@@ -315,38 +340,62 @@
     return jnp.where(row < top, result, 0.0)
 
 
-def run_bins(residual, own, sides, around, masks, parts, weights, gains):
+def run_bins(residual, own, last, sides, around, masks, parts, weights, gains):
     bins, slots, width = residual.shape
-    args = [residual, own, *sides, masks, *parts[0], *parts[1], *weights[1:], *gains]
-
-    def body(residual, own, first, second, masks, *refs):
+    n = len(last)
+    halos = [block for block, _ in last]
+    args = [residual, own, *halos, *sides, masks, *parts[0], *parts[1], *weights[1:], *gains]
+
+    def body(residual, own, *refs):
+        halos, refs = refs[:n], refs[n:]
+        sides, masks, refs = refs[:2], refs[2], refs[3:]
         parts, refs = (refs[:4], refs[4:8]), refs[8:]
-        key_weight, value_weight, *rest, out = refs
-        attended = [
-            attend_role(role, side[...], flag, masks, parts, key_weight, value_weight)
-            for role, side, flag in ((0, first, None), (1, second, inside("gy", around)))
-        ]
-        state = jnp.concatenate([residual[0], residual[1]], axis=0)
-        result = update(state, attended, *rest)
+        key_weight, value_weight = refs[:2]
+        out, done, sems, scratch = refs[7], refs[8], refs[9], refs[10:]
         parity = lax.axis_index("gy") % 2
+        attended = []
         for role in range(ROLES):
-            rows = result[role * slots : (role + 1) * slots]
-            rows = keep_live(rows, own[role, slots : slots + 1, :].astype(F32))
-            out[1 - parity if role == 0 else parity] = rows
+            near = [
+                (halo[role], inside(axis, around)) for halo, (_, axis) in zip(halos, last)
+            ]
+            near.append((sides[role][...], inside("gy", around) if role else None))
+            held = scratch[3 * role : 3 * role + 3]
+            attended.append(
+                attend_role(role, near, masks, parts, key_weight, value_weight, held)
+            )
+        copies = []
+        for role in range(ROLES):
+            rows = update(residual[role], attended[role], refs[2:5], refs[5:7])
+            done[role] = keep_live(rows, own[role, slots : slots + 1, :].astype(F32))
+            target = out.at[1 - parity if role == 0 else parity]
+            copies.append(pltpu.make_async_copy(done.at[role], target, sems.at[role]))
+            copies[-1].start()
+        for copy in copies:
+            copy.wait()
 
     outs = shape((bins, slots, width), F32)
-    return call(body, outs, [VMEM] * len(args))(*args)
-
-
-def run_one(leaving, spans, residual, own, sides, around, masks, parts, weights, gains, places):
+    scratch = [pltpu.VMEM((bins, slots, width), F32), pltpu.SemaphoreType.DMA((ROLES,))]
+    scratch += late_scratch(slots, width, n + 1) * ROLES
+    where = pl.BlockSpec(memory_space=pl.ANY)
+    return call(body, outs, [VMEM] * len(args), scratch, out_specs=where)(*args)
+
+
+def run_one(
+    leaving, spans, residual, own, last, sides, around, masks, parts, weights, gains, places
+):
     _, slots, width = residual.shape
     tall = slots + HEAD_ROWS
-    args = [places, residual, own, *sides, masks, *parts[0], *parts[1], *weights[1:], *gains]
-
-    def body(places, residual, own, first, second, masks, *refs):
+    n = len(last)
+    halos = [block for block, _ in last]
+    args = [residual, own, *halos, *sides, masks, *parts[0], *parts[1], *weights[1:], *gains]
+    args = [places.reshape(1, -1), *args]
+
+    def body(places, residual, own, *refs):
+        halos, refs = refs[:n], refs[n:]
+        first, second, masks, *refs = refs
         parts, refs = (refs[:4], refs[4:8]), refs[8:]
-        key_weight, value_weight, *rest = refs[:7]
-        outs = refs[7:]
+        key_weight, value_weight = refs[:2]
+        outs, scratch = refs[7:-3], refs[-3:]
         parity = lax.axis_index("gy") % 2
         stays = scalar(entry(places[...], 1 - parity)) % spans[1] == lax.axis_index("gz")
         role = jnp.where(stays, 1, 0) if leaving else jnp.where(stays, 0, 1)
@@ -356,8 +405,10 @@
         block = jnp.where(ahead, first[...].astype(F32), second[...].astype(F32)).astype(BF16)
         flag = inside("gy", around)
         flag = flag if flag is None else ahead | flag
-        attended = attend_role(role, block, flag, masks, parts, key_weight, value_weight)
-        result = update(residual[role], [attended], *rest)
+        near = [(halo[role], inside(axis, around)) for halo, (_, axis) in zip(halos, last)]
+        near.append((block, flag))
+        attended = attend_role(role, near, masks, parts, key_weight, value_weight, scratch)
+        result = update(residual[role], attended, refs[2:5], refs[5:7])
         top = own[role, slots:].astype(F32)
         result = keep_live(result, top[:1])
         line = lax.broadcasted_iota(jnp.int32, (HEAD_ROWS, width), 0)
@@ -369,8 +420,7 @@
     outs = [shape((tall, width), BF16)]
     if not leaving:
         outs.append(shape((slots, width), F32))
-    args[0] = places.reshape(1, -1)
-    return call(body, outs, [VMEM] * len(args))(*args)
+    return call(body, outs, [VMEM] * len(args), late_scratch(slots, width, n + 1))(*args)
 
 
 def choose(role, yes, no):
@@ -424,19 +474,20 @@
     return moved, moved_counts
 
 
-def exchange(own, first, second, axes, ends):
-    far = []
-    for axis in axes:
-        for parity in range(2):
-            if not swaps(lax.axis_size(axis), parity):
-                continue
-            how = ends[0] if axis == "gx" else None
-            block = swap(own, axis, parity, how)
-            far.append((block, axis if how and parity == 1 else None))
-    sides = []
-    for parity, block in ((0, first), (1, second)):
-        sides.append(swap(block, "gy", parity, ends[1]))
-    return far, sides
+def exchange(own, first, second, order, ends, last):
+    far, sides = {}, {}
+    for axis, parity in order:
+        if not swaps(lax.axis_size(axis), parity):
+            continue
+        how = {"gx": ends[0], "gy": ends[1]}.get(axis)
+        block = (first, second)[parity] if axis == "gy" else own
+        block = swap(block, axis, parity, how)
+        if axis == "gy":
+            sides[parity] = block
+        else:
+            far[axis, parity] = (block, axis if how and parity == 1 else None)
+    middle = [far[k] for k in sorted(far) if k not in last]
+    return middle, [far[k] for k in sorted(far) if k in last], [sides[0], sides[1]]
 
 
 def shards(features, occupancy, dest_bin, *rest):
@@ -448,31 +499,32 @@
     depth = lax.axis_size("gz")
     spans = (2 * lax.axis_size("gy"), depth)
 
-    def finish(own, residual, beside, far, sides, ends):
+    def finish(own, residual, beside, far, last, sides, ends):
         around = bool(ends[1])
         masks, first = run_early(own, beside, weights)
         second = run_middle(far, masks, weights, True)
-        return residual, own, sides, around, masks, (first, second), weights, gains
+        return residual, own, last, sides, around, masks, (first, second), weights, gains
 
     ready = prepare(slots, width)
     own, first, second, residual = pack(state, counts, ready)
-    far, sides = exchange(own, first, second, ("gx", "gz"), ENDS[0])
-    known = finish(own, residual, [], far, sides, ENDS[0])
+    far = exchange(own, first, second, ORDERS[0], ENDS[0], LAST[0])
+    known = finish(own, residual, [], *far, ENDS[0])
     if depth == 2:
         (leave,) = run_one(True, spans, *known, places)
         came = swap(leave, "gz", 0, None)
         stay, stayed = run_one(False, spans, *known, places)
         peer = swap(stay, "gz", 0, None)
         own, first, second, residual = settle(stay, stayed, came)
-        beside, axes = [peer, leave], ("gx",)
+        beside = [peer, leave]
+        order = [k for k in ORDERS[1] if k[0] != "gz"]
     else:
         state = run_bins(*known)
     if depth != 2:
         state, counts = relocate(state, counts, places, 2)
         own, first, second, residual = pack(state, counts, ready)
-        beside, axes = [], ("gx", "gz")
-    far, sides = exchange(own, first, second, axes, ENDS[1])
-    out = run_bins(*finish(own, residual, beside, far, sides, ENDS[1]))
+        beside, order = [], ORDERS[1]
+    far = exchange(own, first, second, order, ENDS[1], LAST[1])
+    out = run_bins(*finish(own, residual, beside, *far, ENDS[1]))
     return out.reshape(features.shape)
 
 

time: 35.4 us -> 33.3 us (0.941)
  starting transfers between devices: 16.7 us -> 14.8 us
  Pallas kernels: 12.8 us -> 12.3 us
    ppermute x11, starting transfers between devices: 16.7 us -> 14.8 us  [swap(): return lax.ppermute(block, axis, pairs)]
    pallas_call x2, Pallas kernels: 2.08 us -> 1.34 us  [run_middle(): return call(body, part_shapes(slots, width, n), [VMEM] * len(args))(*args)]
where the time goes in v1:
time: 33.3 us; the launch traced here: 33.1 us
  starting transfers between devices  14.8 us (44%)
  Pallas kernels  12.3 us (37%)
  waiting for transfers between devices  4.85 us (15%)
  local copies, waits for them, and re-layouts  0.92 us (3%)
    ppermute x11, starting transfers between devices, swap(): return lax.ppermute(block, axis, pairs)  14.8 us
    ppermute x11, waiting for transfers between devices, swap(): return lax.ppermute(block, axis, pairs)  4.85 us
    pallas_call x2, Pallas kernels, run_one(): call(body, outs, [VMEM] * len(args), late_scratch(slots, width, n + 1))  4.47 us
    pallas_call x1, Pallas kernels, run_bins(): return call(body, outs, [VMEM] * len(args), scratch, out_specs=where)(*args)  4.04 us
    pallas_call x2, Pallas kernels, run_early(): masks, *part = call(body, outs, [VMEM] * len(args))(*args)  2.29 us
    pallas_call x2, Pallas kernels, run_middle(): return call(body, part_shapes(slots, width, n), [VMEM] * len(args))(*args)  1.34 us
    unnamed x22, local copies, waits for them, and re-layouts  0.92 us
  transfers between devices with their start and end apart: 11, of which 3 were waited for; matrix products, arithmetic and copies ran while one was open for 0% of the time, Pallas kernels for 18%

profile of v1, /device:TPU:0, one launch (start us, length us, event | category | flops | bytes accessed | tf_op | source)
XLA Modules:
  0.0 33.1 jit_solution(18174617892509820332)
XLA Ops:
  0.0 0.0 copy-start.10
  0.0 0.0 copy-start.6
  0.0 0.0 copy-start.1
  0.0 0.0 copy-start
  0.0 0.0 copy-start.5
  0.0 0.0 copy-start.3
  0.0 0.0 copy-start.2
  0.0 0.0 copy-start.4
  0.0 0.0 copy-start.8
  0.1 0.0 copy-start.7
  0.1 0.0 copy-start.9
  0.1 0.6 %copy-done.10 = s32[1,2,1]{1,2,0:T(1,128)S(1)} copy-done((s32[1,2,1]{1,2,0:T(1,128)S(1)}, s32[1,2,1]{1,2,0:T(1,128)}, u32[]{:S(2)}) %copy-start.10) | copy-done | bytes 32
  0.7 0.3 copy-done.6
  1.0 0.1 shard_map.109
  1.1 3.1 %collective-permute-start.4 = (bf16[2,144,256]{2,1,0:T(8,128)(2,1)S(1)}, bf16[2,144,256]{2,1,0:T(8,128)(2,1)S(1)}, u32[]{:S(2)}, u32[]{:S(2)}) collective-permute-start(bf16[2,144,256]{2,1,0:T(8,128)(2,1)S(1)} %get-tuple-element.34.own), channel_id=1, source_target_pairs={{0,8},{8,0},{16,24},{24,16},{1,9},{9,1},{17,25},{25,17},{2,10},{10... | collective-permute-start | bytes 442376 | tf_op jit(solution)/shard_map/ppermute | solution.py:70
  4.2 1.5 %collective-permute-start.1 = (bf16[2,144,256]{2,1,0:T(8,128)(2,1)S(1)}, bf16[2,144,256]{2,1,0:T(8,128)(2,1)S(1)}, u32[]{:S(2)}, u32[]{:S(2)}) collective-permute-start(bf16[2,144,256]{2,1,0:T(8,128)(2,1)S(1)} %get-tuple-element.34.own), channel_id=1, source_target_pairs={{0,1},{1,0},{2,3},{3,2},{4,5},{5,4},{6,7},{7,6},{8,9},{9,8},{10,11... | collective-permute-start | bytes 442376 | tf_op jit(solution)/shard_map/ppermute | solution.py:70
  5.7 0.7 %collective-permute-start = (bf16[2,144,256]{2,1,0:T(8,128)(2,1)S(1)}, bf16[2,144,256]{2,1,0:T(8,128)(2,1)S(1)}, u32[]{:S(2)}, u32[]{:S(2)}) collective-permute-start(bf16[2,144,256]{2,1,0:T(8,128)(2,1)S(1)} %get-tuple-element.34.own), channel_id=1, source_target_pairs={{8,16},{16,8},{9,17},{17,9},{10,18},{18,10},{11,19},{19,11},{12,20... | collective-permute-start | bytes 442376 | tf_op jit(solution)/shard_map/ppermute | solution.py:70
  6.4 0.1 collective-permute-start.2
  6.4 1.6 %collective-permute-start.3 = (bf16[144,256]{1,0:T(8,128)(2,1)S(1)}, bf16[144,256]{1,0:T(8,128)(2,1)S(1)}, u32[]{:S(2)}, u32[]{:S(2)}) collective-permute-start(bf16[144,256]{1,0:T(8,128)(2,1)S(1)} %get-tuple-element.36), channel_id=1, source_target_pairs={{2,4},{4,2},{0,6},{6,0},{3,5},{5,3},{1,7},{7,1},{10,12},{12,10},{8... | collective-permute-start | bytes 221192 | tf_op jit(solution)/shard_map/ppermute | solution.py:70
  8.0 0.0 copy-done.1
  8.0 0.0 copy-done
  8.0 0.0 copy-done.5
  8.0 1.0 %shard_map.110 = (bf16[8,256,256]{2,1,0:T(8,128)(2,1)S(1)}, bf16[2,256,256]{2,1,0:T(8,128)(2,1)S(1)}, f32[8,256,256]{2,1,0:T(8,128)S(1)}, f32[8,1,256]{2,1,0:T(1,128)S(1)}, f32[8,1,256]{2,1,0:T(1,128)S(1)}) custom-call(bf16[2,144,256]{2,1,0:T(8,128)(2,1)S(1)} %get-tuple-element.34.own, bf16[256,256]{1,0:T(8,128)(2,1)S(1)} %copy-done.5, ...), custom_call_target="tpu_custom_call" | custom-call | tf_op jit(solution)/shard_map/pallas_call | solution.py:236
  9.0 0.0 collective-permute-done.4.refs_0_
  9.0 0.7 %shard_map.111 = (bf16[2,256,128]{2,1,0:T(8,128)(2,1)S(1)}, f32[8,128,256]{2,1,0:T(8,128)S(1)}, f32[8,1,256]{2,1,0:T(1,128)S(1)}, f32[8,1,256]{2,1,0:T(1,128)S(1)}) custom-call(bf16[2,144,256]{2,1,0:T(8,128)(2,1)S(1)} %collective-permute-done.4.refs_0_, bf16[8,256,256]{2,1,0:T(8,128)(2,1)S(1)} %get-tuple-element.37.refs_1_.refs_4_, ...), custom_call_target="tpu_custom_call" | custom-call | tf_op jit(solution)/shard_map/pallas_call | solution.py:267
  9.7 0.0 collective-permute-done.2.refs_2_
  9.7 0.8 %collective-permute-done.3.refs_3_ = bf16[144,256]{1,0:T(8,128)(2,1)S(1)} collective-permute-done((bf16[144,256]{1,0:T(8,128)(2,1)S(1)}, bf16[144,256]{1,0:T(8,128)(2,1)S(1)}, u32[]{:S(2)}, u32[]{:S(2)}) %collective-permute-start.3) | collective-permute-done | bytes 73760 | tf_op jit(solution)/shard_map/ppermute | solution.py:70
  10.5 0.0 collective-permute-done.1.refs_1_
  10.5 0.0 collective-permute-done.refs_0_
  10.5 0.0 copy-done.3
  10.5 0.0 copy-done.2
  10.5 0.0 copy-done.4
  10.5 0.0 copy-done.8
  10.5 0.0 copy-done.7
  10.5 0.0 copy-done.9
  10.5 2.2 %shard_map.113.refs_1_ = bf16[144,256]{1,0:T(8,128)(2,1)S(1)} custom-call(s32[1,2]{1,0:T(1,128)S(1)} %bitcast.15, f32[2,128,256]{2,1,0:T(8,128)S(1)} %get-tuple-element.33.residual, bf16[2,144,256]{2,1,0:T(8,128)(2,1)S(1)} %get-tuple-element.34.own, bf16[2,144,256]{2,1,0:T(8,128)(2,1)S(1)} %collective-permute-done.refs_0_, ...), custom_call_target="tpu_custom_call" | custom-call | tf_op jit(solution)/shard_map/pallas_call | solution.py:423
  12.8 0.6 %collective-permute-start.5 = (bf16[144,256]{1,0:T(8,128)(2,1)S(1)}, bf16[144,256]{1,0:T(8,128)(2,1)S(1)}, u32[]{:S(2)}, u32[]{:S(2)}) collective-permute-start(bf16[144,256]{1,0:T(8,128)(2,1)S(1)} %shard_map.113.refs_1_), channel_id=1, source_target_pairs={{0,1},{1,0},{2,3},{3,2},{4,5},{5,4},{6,7},{7,6},{8,9},{9,8},{10,11... | collective-permute-start | bytes 221192 | tf_op jit(solution)/shard_map/ppermute | solution.py:70
  13.4 2.2 %shard_map.112 = (bf16[144,256]{1,0:T(8,128)(2,1)S(1)}, f32[128,256]{1,0:T(8,128)S(1)}) custom-call(s32[1,2]{1,0:T(1,128)S(1)} %bitcast.16, f32[2,128,256]{2,1,0:T(8,128)S(1)} %get-tuple-element.33.residual, bf16[2,144,256]{2,1,0:T(8,128)(2,1)S(1)} %get-tuple-element.34.own, bf16[2,144,256]{2,1,0:T(8,128)(2,1)S(1)} %collective-permute-done.refs_0_, ...), custom_call_target="tpu_custom_call" | custom-call | tf_op jit(solution)/shard_map/pallas_call | solution.py:423
  15.6 1.8 %collective-permute-done.5.came = bf16[144,256]{1,0:T(8,128)(2,1)S(1)} collective-permute-done((bf16[144,256]{1,0:T(8,128)(2,1)S(1)}, bf16[144,256]{1,0:T(8,128)(2,1)S(1)}, u32[]{:S(2)}, u32[]{:S(2)}) %collective-permute-start.5) | collective-permute-done | bytes 73760 | tf_op jit(solution)/shard_map/ppermute | solution.py:70
  17.4 0.1 shard_map.114
  17.5 4.5 %collective-permute-start.10 = (bf16[2,144,256]{2,1,0:T(8,128)(2,1)S(1)}, bf16[2,144,256]{2,1,0:T(8,128)(2,1)S(1)}, u32[]{:S(2)}, u32[]{:S(2)}) collective-permute-start(bf16[2,144,256]{2,1,0:T(8,128)(2,1)S(1)} %get-tuple-element.49.own), channel_id=1, source_target_pairs={{0,8},{8,0},{16,24},{24,16},{1,9},{9,1},{17,25},{25,17},{2,10},{10... | collective-permute-start | bytes 442376 | tf_op jit(solution)/shard_map/ppermute | solution.py:70
  21.9 0.7 %collective-permute-start.6 = (bf16[2,144,256]{2,1,0:T(8,128)(2,1)S(1)}, bf16[2,144,256]{2,1,0:T(8,128)(2,1)S(1)}, u32[]{:S(2)}, u32[]{:S(2)}) collective-permute-start(bf16[2,144,256]{2,1,0:T(8,128)(2,1)S(1)} %get-tuple-element.49.own), channel_id=1, source_target_pairs={{8,16},{16,8},{9,17},{17,9},{10,18},{18,10},{11,19},{19,11},{12,20... | collective-permute-start | bytes 442376 | tf_op jit(solution)/shard_map/ppermute | solution.py:70
  22.6 0.6 %collective-permute-start.9 = (bf16[144,256]{1,0:T(8,128)(2,1)S(1)}, bf16[144,256]{1,0:T(8,128)(2,1)S(1)}, u32[]{:S(2)}, u32[]{:S(2)}) collective-permute-start(bf16[144,256]{1,0:T(8,128)(2,1)S(1)} %get-tuple-element.46.stay), channel_id=1, source_target_pairs={{0,1},{1,0},{2,3},{3,2},{4,5},{5,4},{6,7},{7,6},{8,9},{9,8},{10,11... | collective-permute-start | bytes 221192 | tf_op jit(solution)/shard_map/ppermute | solution.py:70
  23.2 0.0 collective-permute-start.7
  23.2 1.6 %collective-permute-start.8 = (bf16[144,256]{1,0:T(8,128)(2,1)S(1)}, bf16[144,256]{1,0:T(8,128)(2,1)S(1)}, u32[]{:S(2)}, u32[]{:S(2)}) collective-permute-start(bf16[144,256]{1,0:T(8,128)(2,1)S(1)} %get-tuple-element.51), channel_id=1, source_target_pairs={{2,4},{4,2},{0,6},{6,0},{3,5},{5,3},{1,7},{7,1},{10,12},{12,10},{8... | collective-permute-start | bytes 221192 | tf_op jit(solution)/shard_map/ppermute | solution.py:70
  24.8 2.2 %collective-permute-done.9.refs_0_ = bf16[144,256]{1,0:T(8,128)(2,1)S(1)} collective-permute-done((bf16[144,256]{1,0:T(8,128)(2,1)S(1)}, bf16[144,256]{1,0:T(8,128)(2,1)S(1)}, u32[]{:S(2)}, u32[]{:S(2)}) %collective-permute-start.9) | collective-permute-done | bytes 73760 | tf_op jit(solution)/shard_map/ppermute | solution.py:70
  27.0 1.3 %shard_map.115 = (bf16[8,256,256]{2,1,0:T(8,128)(2,1)S(1)}, bf16[2,256,384]{2,1,0:T(8,128)(2,1)S(1)}, f32[8,384,256]{2,1,0:T(8,128)S(1)}, f32[8,1,256]{2,1,0:T(1,128)S(1)}, f32[8,1,256]{2,1,0:T(1,128)S(1)}) custom-call(bf16[2,144,256]{2,1,0:T(8,128)(2,1)S(1)} %get-tuple-element.49.own, bf16[144,256]{1,0:T(8,128)(2,1)S(1)} %collective-permute-done.9.refs_0_, ...), custom_call_target="tpu_custom_call" | custom-call | tf_op jit(solution)/shard_map/pallas_call | solution.py:236
  28.4 0.0 collective-permute-done.10.refs_0_
  28.4 0.7 %shard_map.116 = (bf16[2,256,128]{2,1,0:T(8,128)(2,1)S(1)}, f32[8,128,256]{2,1,0:T(8,128)S(1)}, f32[8,1,256]{2,1,0:T(1,128)S(1)}, f32[8,1,256]{2,1,0:T(1,128)S(1)}) custom-call(bf16[2,144,256]{2,1,0:T(8,128)(2,1)S(1)} %collective-permute-done.10.refs_0_, bf16[8,256,256]{2,1,0:T(8,128)(2,1)S(1)} %get-tuple-element.52.refs_1_.refs_3_, ...), custom_call_target="tpu_custom_call" | custom-call | tf_op jit(solution)/shard_map/pallas_call | solution.py:267
  29.0 0.0 collective-permute-done.7.refs_1_
  29.1 0.0 collective-permute-done.8.refs_2_
  29.1 0.0 collective-permute-done.6.refs_0_
  29.1 4.0 %shard_map.117 = f32[2,128,256]{2,1,0:T(8,128)} custom-call(f32[2,128,256]{2,1,0:T(8,128)S(1)} %get-tuple-element.48.residual, bf16[2,144,256]{2,1,0:T(8,128)(2,1)S(1)} %get-tuple-element.49.own, bf16[2,144,256]{2,1,0:T(8,128)(2,1)S(1)} %collective-permute-done.6.refs_0_, bf16[144,256]{1,0:T(8,128)(2,1)S(1)} %collective-permute-done.7.refs_1_, ...), custom_call_target="tpu_custom_call" | custom-call | tf_op jit(solution)/shard_map/pallas_call | solution.py:380
  (1 shorter events, 0.0 us)
Async XLA Ops:
  0.0 0.7 %copy-start.10 = (s32[1,2,1]{1,2,0:T(1,128)S(1)}, s32[1,2,1]{1,2,0:T(1,128)}, u32[]{:S(2)}) copy-start(s32[1,2,1]{1,2,0:T(1,128)} %param.12) | copy-start | bytes 28
  0.0 1.0 %copy-start.6 = (f32[1,2,1,128,256]{4,3,2,1,0:T(8,128)S(1)}, f32[1,2,1,128,256]{4,3,2,1,0:T(8,128)}, u32[]{:S(2)}) copy-start(f32[1,2,1,128,256]{4,3,2,1,0:T(8,128)} %param.11) | copy-start | bytes 786436
  0.0 8.0 %copy-start.1 = (bf16[256,256]{1,0:T(8,128)(2,1)S(1)}, bf16[256,256]{1,0:T(8,128)(2,1)}, u32[]{:S(2)}) copy-start(bf16[256,256]{1,0:T(8,128)(2,1)} %refs_13_.5) | copy-start | bytes 393220
  0.0 8.0 %copy-start = (bf16[256,256]{1,0:T(8,128)(2,1)S(1)}, bf16[256,256]{1,0:T(8,128)(2,1)}, u32[]{:S(2)}) copy-start(bf16[256,256]{1,0:T(8,128)(2,1)} %refs_12_.1) | copy-start | bytes 393220
  0.0 8.0 %copy-start.5 = (bf16[256,256]{1,0:T(8,128)(2,1)S(1)}, bf16[256,256]{1,0:T(8,128)(2,1)}, u32[]{:S(2)}) copy-start(bf16[256,256]{1,0:T(8,128)(2,1)} %refs_2_.6) | copy-start | bytes 393220
  0.0 10.4 %copy-start.3 = (bf16[1024,256]{1,0:T(8,128)(2,1)S(1)}, bf16[1024,256]{1,0:T(8,128)(2,1)}, u32[]{:S(2)}) copy-start(bf16[1024,256]{1,0:T(8,128)(2,1)} %refs_16_.5) | copy-start | bytes 1572868
  0.0 10.4 %copy-start.2 = (bf16[256,1024]{1,0:T(8,128)(2,1)S(1)}, bf16[256,1024]{1,0:T(8,128)(2,1)}, u32[]{:S(2)}) copy-start(bf16[256,1024]{1,0:T(8,128)(2,1)} %refs_15_.5) | copy-start | bytes 1572868
  0.0 10.4 %copy-start.4 = (bf16[256,256]{1,0:T(8,128)(2,1)S(1)}, bf16[256,256]{1,0:T(8,128)(2,1)}, u32[]{:S(2)}) copy-start(bf16[256,256]{1,0:T(8,128)(2,1)} %refs_14_.5) | copy-start | bytes 393220
  0.0 10.4 %copy-start.8 = (f32[256]{0:T(256)S(1)}, f32[256]{0:T(256)}, u32[]{:S(2)}) copy-start(f32[256]{0:T(256)} %param.21) | copy-start | bytes 3076
  0.1 10.4 %copy-start.7 = (f32[256]{0:T(256)S(1)}, f32[256]{0:T(256)}, u32[]{:S(2)}) copy-start(f32[256]{0:T(256)} %param.20) | copy-start | bytes 3076
  0.1 10.4 %copy-start.9 = (s32[1,2,1]{1,2,0:T(1,128)S(1)}, s32[1,2,1]{1,2,0:T(1,128)}, u32[]{:S(2)}) copy-start(s32[1,2,1]{1,2,0:T(1,128)} %param.13) | copy-start | bytes 28
  1.1 7.9 %collective-permute-start.4 = (bf16[2,144,256]{2,1,0:T(8,128)(2,1)S(1)}, bf16[2,144,256]{2,1,0:T(8,128)(2,1)S(1)}, u32[]{:S(2)}, u32[]{:S(2)}) collective-permute-start(bf16[2,144,256]{2,1,0:T(8,128)(2,1)S(1)} %get-tuple-element.34.own), channel_id=1, source_target_pairs={{0,8},{8,0},{16,24},{24,16},{1,9},{9,1},{17,25},{25,17},{2,10},{10... | collective-permute-start | bytes 442376 | tf_op jit(solution)/shard_map/ppermute | solution.py:70
  4.2 6.3 %collective-permute-start.1 = (bf16[2,144,256]{2,1,0:T(8,128)(2,1)S(1)}, bf16[2,144,256]{2,1,0:T(8,128)(2,1)S(1)}, u32[]{:S(2)}, u32[]{:S(2)}) collective-permute-start(bf16[2,144,256]{2,1,0:T(8,128)(2,1)S(1)} %get-tuple-element.34.own), channel_id=1, source_target_pairs={{0,1},{1,0},{2,3},{3,2},{4,5},{5,4},{6,7},{7,6},{8,9},{9,8},{10,11... | collective-permute-start | bytes 442376 | tf_op jit(solution)/shard_map/ppermute | solution.py:70
  5.7 4.8 %collective-permute-start = (bf16[2,144,256]{2,1,0:T(8,128)(2,1)S(1)}, bf16[2,144,256]{2,1,0:T(8,128)(2,1)S(1)}, u32[]{:S(2)}, u32[]{:S(2)}) collective-permute-start(bf16[2,144,256]{2,1,0:T(8,128)(2,1)S(1)} %get-tuple-element.34.own), channel_id=1, source_target_pairs={{8,16},{16,8},{9,17},{17,9},{10,18},{18,10},{11,19},{19,11},{12,20... | collective-permute-start | bytes 442376 | tf_op jit(solution)/shard_map/ppermute | solution.py:70
  6.4 3.3 %collective-permute-start.2 = (bf16[144,256]{1,0:T(8,128)(2,1)S(1)}, bf16[144,256]{1,0:T(8,128)(2,1)S(1)}, u32[]{:S(2)}, u32[]{:S(2)}) collective-permute-start(bf16[144,256]{1,0:T(8,128)(2,1)S(1)} %get-tuple-element.35), channel_id=1, source_target_pairs={{0,2},{2,0},{4,6},{6,4},{1,3},{3,1},{5,7},{7,5},{8,10},{10,8},{12,... | collective-permute-start | bytes 221192 | tf_op jit(solution)/shard_map/ppermute | solution.py:70
  6.4 4.0 %collective-permute-start.3 = (bf16[144,256]{1,0:T(8,128)(2,1)S(1)}, bf16[144,256]{1,0:T(8,128)(2,1)S(1)}, u32[]{:S(2)}, u32[]{:S(2)}) collective-permute-start(bf16[144,256]{1,0:T(8,128)(2,1)S(1)} %get-tuple-element.36), channel_id=1, source_target_pairs={{2,4},{4,2},{0,6},{6,0},{3,5},{5,3},{1,7},{7,1},{10,12},{12,10},{8... | collective-permute-start | bytes 221192 | tf_op jit(solution)/shard_map/ppermute | solution.py:70
  12.8 4.7 %collective-permute-start.5 = (bf16[144,256]{1,0:T(8,128)(2,1)S(1)}, bf16[144,256]{1,0:T(8,128)(2,1)S(1)}, u32[]{:S(2)}, u32[]{:S(2)}) collective-permute-start(bf16[144,256]{1,0:T(8,128)(2,1)S(1)} %shard_map.113.refs_1_), channel_id=1, source_target_pairs={{0,1},{1,0},{2,3},{3,2},{4,5},{5,4},{6,7},{7,6},{8,9},{9,8},{10,11... | collective-permute-start | bytes 221192 | tf_op jit(solution)/shard_map/ppermute | solution.py:70
  17.5 10.9 %collective-permute-start.10 = (bf16[2,144,256]{2,1,0:T(8,128)(2,1)S(1)}, bf16[2,144,256]{2,1,0:T(8,128)(2,1)S(1)}, u32[]{:S(2)}, u32[]{:S(2)}) collective-permute-start(bf16[2,144,256]{2,1,0:T(8,128)(2,1)S(1)} %get-tuple-element.49.own), channel_id=1, source_target_pairs={{0,8},{8,0},{16,24},{24,16},{1,9},{9,1},{17,25},{25,17},{2,10},{10... | collective-permute-start | bytes 442376 | tf_op jit(solution)/shard_map/ppermute | solution.py:70
  21.9 7.1 %collective-permute-start.6 = (bf16[2,144,256]{2,1,0:T(8,128)(2,1)S(1)}, bf16[2,144,256]{2,1,0:T(8,128)(2,1)S(1)}, u32[]{:S(2)}, u32[]{:S(2)}) collective-permute-start(bf16[2,144,256]{2,1,0:T(8,128)(2,1)S(1)} %get-tuple-element.49.own), channel_id=1, source_target_pairs={{8,16},{16,8},{9,17},{17,9},{10,18},{18,10},{11,19},{19,11},{12,20... | collective-permute-start | bytes 442376 | tf_op jit(solution)/shard_map/ppermute | solution.py:70
  22.6 4.4 %collective-permute-start.9 = (bf16[144,256]{1,0:T(8,128)(2,1)S(1)}, bf16[144,256]{1,0:T(8,128)(2,1)S(1)}, u32[]{:S(2)}, u32[]{:S(2)}) collective-permute-start(bf16[144,256]{1,0:T(8,128)(2,1)S(1)} %get-tuple-element.46.stay), channel_id=1, source_target_pairs={{0,1},{1,0},{2,3},{3,2},{4,5},{5,4},{6,7},{7,6},{8,9},{9,8},{10,11... | collective-permute-start | bytes 221192 | tf_op jit(solution)/shard_map/ppermute | solution.py:70
  23.2 5.9 %collective-permute-start.7 = (bf16[144,256]{1,0:T(8,128)(2,1)S(1)}, bf16[144,256]{1,0:T(8,128)(2,1)S(1)}, u32[]{:S(2)}, u32[]{:S(2)}) collective-permute-start(bf16[144,256]{1,0:T(8,128)(2,1)S(1)} %get-tuple-element.50), channel_id=1, source_target_pairs={{0,2},{2,0},{4,6},{6,4},{1,3},{3,1},{5,7},{7,5},{8,10},{10,8},{12,... | collective-permute-start | bytes 221192 | tf_op jit(solution)/shard_map/ppermute | solution.py:70
  23.2 5.9 %collective-permute-start.8 = (bf16[144,256]{1,0:T(8,128)(2,1)S(1)}, bf16[144,256]{1,0:T(8,128)(2,1)S(1)}, u32[]{:S(2)}, u32[]{:S(2)}) collective-permute-start(bf16[144,256]{1,0:T(8,128)(2,1)S(1)} %get-tuple-element.51), channel_id=1, source_target_pairs={{2,4},{4,2},{0,6},{6,0},{3,5},{5,3},{1,7},{7,1},{10,12},{12,10},{8... | collective-permute-start | bytes 221192 | tf_op jit(solution)/shard_map/ppermute | solution.py:70
